TPU v7x, 32 devices: a whole 2x2x4 slice. The times are simulated.
32 devices in a mesh: seq: 4 (over y, x), ep: 8 (over z, core).
Axes of the slice: x: 2, y: 2, z: 4, core: 2. Of those that a mesh axis runs over, the one named last changes fastest.
Arguments:
- tokens: bfloat16 [24, 576, 768], P('ep', 'seq'), may hold values from -6 to 6
- routes: int32 [24, 576, 2], P('ep', 'seq'), may hold values from 0 to 31, all different within a row
- priority: int32 [24, 576], P('ep', 'seq'), may hold values from 0 to 431, as said below
- hires: int32 [8], P('ep'), may hold values from 0 to 3
- gain_one: float32 [768], replicated, may hold values from 0.1 to 1.9
- shift_one: float32 [768], replicated, may hold values from -1.8 to 1.8
- w_qkv: bfloat16 [768, 2304], replicated, may hold values from -0.21875 to 0.21875
- w_proj: bfloat16 [768, 768], replicated, may hold values from -6 to 6
- gain_two: float32 [768], replicated, may hold values from 0.1 to 1.9
- shift_two: float32 [768], replicated, may hold values from -1.8 to 1.8
- w_router: bfloat16 [768, 32], replicated, may hold values from -0.15917969 to 0.15917969
- expert_in: bfloat16 [98304, 768], P('ep'), may hold values from -0.21875 to 0.21875
- expert_out: bfloat16 [98304, 768], P('ep'), may hold values from -2.5 to 2.5
- cotangent: bfloat16 [24, 576, 768], P('ep', 'seq'), may hold values from -6 to 6
Outputs:
- output: bfloat16 [24, 576, 768], P('ep', 'seq')
- input_grad: bfloat16 [24, 576, 768], P('ep', 'seq')
- gain_one_grad: float32 [768], replicated
- shift_one_grad: float32 [768], replicated
- qkv_grad: float32 [768, 2304], replicated
- proj_grad: float32 [768, 768], replicated
- gain_two_grad: float32 [768], replicated
- shift_two_grad: float32 [768], replicated
- router_grad: float32 [768, 32], replicated
- expert_in_grad: float32 [98304, 768], P('ep')
- expert_out_grad: float32 [98304, 768], P('ep')
- rms_stats: float32 [3], replicated
Inputs may be any that keep to these rules, and one draw needn't show every extreme that they name: `priority`: within each device block of 3 images times 144 positions, the priorities are a permutation of 0 to 431.
All inputs are finite; a program needn't handle non-finite values.
Results may differ from a plain program's by a relative error of at most 0.015.
Values may be sent and summed in bfloat16 or wider, within the bound.
No kernel may reach another device: no remote copies, remote signals or barrier semaphores. Data moves between devices by JAX's collectives and lax.ppermute only.
A program may use at most 320 MiB of HBM per device.

v0:
```python
import jax
import jax.numpy as jnp
from jax import lax
from jax.sharding import PartitionSpec as P

HEADS = 12
EXPERTS = 32
TOP = 2
PATCHES = 576
SHORT = 196
norm_eps = 1e-06
neg_big = -1e30


def norm_forward(values, norm_gain, norm_bias):
    row_mean = jnp.mean(values, axis=-1, keepdims=True)
    centred = values - row_mean
    inv_root = lax.rsqrt(jnp.mean(centred * centred, axis=-1, keepdims=True) + norm_eps)
    normed = centred * inv_root
    return (normed * norm_gain + norm_bias, normed, inv_root)


def norm_backward(grad_out, normed, inv_root, norm_gain):
    gain_grad = jnp.sum(grad_out * normed, axis=0)
    bias_grad = jnp.sum(grad_out, axis=0)
    scaled = grad_out * norm_gain
    grad_in = inv_root * (
        scaled
        - jnp.mean(scaled, axis=-1, keepdims=True)
        - normed * jnp.mean(scaled * normed, axis=-1, keepdims=True)
    )
    return (grad_in, gain_grad, bias_grad)


def gelu_slope(values):
    return (
        0.5 * (1.0 + lax.erf(values * 0.7071067811865476))
        + values * jnp.exp(-0.5 * values * values) * 0.3989422804014327
    )


def routing(route_rows, priority_rows, row_valid, capacity):
    row_total = route_rows.shape[0]
    by_priority = (
        jnp.zeros((row_total,), jnp.int32)
        .at[priority_rows]
        .set(jnp.arange(row_total, dtype=jnp.int32))
    )
    ordered = jnp.concatenate([route_rows[by_priority, route_rank] for route_rank in range(TOP)])
    ordered_valid = jnp.concatenate([row_valid[by_priority]] * TOP)
    expert_hits = (
        ordered[:, None] == jnp.arange(EXPERTS, dtype=jnp.int32)[None, :]
    ) & ordered_valid[:, None]
    running = jnp.cumsum(expert_hits.astype(jnp.int32), axis=0)
    ordered_slot = jnp.sum(jnp.where(expert_hits, running, 0), axis=1) - 1
    pair_slot = ordered_slot.reshape(TOP, row_total)[:, priority_rows].T
    is_kept = (pair_slot >= 0) & (pair_slot < capacity)
    return jnp.where(is_kept, route_rows * capacity + pair_slot, EXPERTS * capacity)


def slot_sources(slot_dest, fill_value, capacity, divisor):
    flat_dest = slot_dest.reshape(-1)
    source_ids = jnp.arange(flat_dest.shape[0], dtype=jnp.int32) // divisor
    table_ids = (
        jnp.full((EXPERTS * capacity + 1,), fill_value, jnp.int32).at[flat_dest].set(source_ids)
    )
    return table_ids[: EXPERTS * capacity]


def fan_out(slot_table, ep_count, split_count, local_experts, capacity):
    feature_width = slot_table.shape[-1]
    grouped = slot_table.reshape(ep_count // split_count, 1, local_experts, capacity, feature_width)
    spread = jnp.broadcast_to(
        grouped, (ep_count // split_count, split_count, local_experts, capacity, feature_width)
    )
    return spread.reshape(ep_count, local_experts, capacity, feature_width)


def fan_in(arrived, split_count):
    ep_count, local_experts, capacity, feature_width = arrived.shape
    grouped = arrived.reshape(
        ep_count // split_count, split_count, local_experts, capacity, feature_width
    )
    return jnp.sum(grouped.astype(jnp.float32), axis=1).reshape(-1, feature_width)


def score_block(query_heads, key_heads, key_mask, score_scale):
    raw_scores = (
        jnp.einsum("ishd,ithd->ihst", query_heads, key_heads, preferred_element_type=jnp.float32)
        * score_scale
    )
    return jnp.where(key_mask[:, None, None, :], raw_scores, neg_big)


def per_device(
    tokens,
    routes,
    priority,
    hires,
    gain_one,
    shift_one,
    w_qkv,
    w_proj,
    gain_two,
    shift_two,
    w_router,
    expert_in,
    expert_out,
    cotangent,
):
    image_count, patch_rows, model_width = tokens.shape
    row_count = image_count * patch_rows
    seq_count = lax.axis_size("seq")
    ep_count = lax.axis_size("ep")
    full_patches = patch_rows * seq_count
    head_width = model_width // HEADS
    score_scale = head_width ** (-0.5)
    local_experts = max(1, EXPERTS // ep_count)
    split_count = max(1, ep_count // EXPERTS)
    local_hidden = expert_in.shape[0] // local_experts
    capacity = max(2, (105 * TOP * row_count + 100 * EXPERTS - 1) // (100 * EXPERTS))
    seq_place = lax.axis_index("seq")

    def send_slots(slot_table):
        outgoing = fan_out(slot_table, ep_count, split_count, local_experts, capacity)
        return lax.all_to_all(outgoing, "ep", split_axis=0, concat_axis=0, tiled=True)

    def return_slots(part_rows):
        returned = lax.all_to_all(part_rows, "ep", split_axis=0, concat_axis=0, tiled=True)
        return fan_in(returned, split_count)

    image_length = jnp.where(jnp.arange(image_count, dtype=jnp.int32) < hires[0], PATCHES, SHORT)
    key_mask = jnp.arange(full_patches, dtype=jnp.int32)[None, :] < image_length[:, None]
    own_mask = (seq_place * patch_rows + jnp.arange(patch_rows, dtype=jnp.int32))[
        None, :
    ] < image_length[:, None]
    row_valid = own_mask.reshape(row_count)
    valid_col = row_valid.astype(jnp.float32)[:, None]
    inputs = tokens.reshape(row_count, model_width).astype(jnp.float32)
    head_shape = (image_count, -1, HEADS, head_width)
    first_out, normed_one, inv_one = norm_forward(inputs, gain_one, shift_one)
    attn_in = first_out.astype(jnp.bfloat16)
    packed = jnp.dot(attn_in, w_qkv, preferred_element_type=jnp.float32).astype(jnp.bfloat16)
    query_rows = packed[:, :model_width].reshape(image_count, patch_rows, model_width)
    key_rows = packed[:, model_width : 2 * model_width].reshape(
        image_count, patch_rows, model_width
    )
    value_rows = packed[:, 2 * model_width :].reshape(image_count, patch_rows, model_width)
    query_heads = query_rows.reshape(head_shape)
    keys_all, values_all = (
        lax.all_gather(key_rows, "seq", axis=1, tiled=True),
        lax.all_gather(value_rows, "seq", axis=1, tiled=True),
    )
    scores = score_block(query_heads, keys_all.reshape(head_shape), key_mask, score_scale)
    row_max = jnp.max(scores, axis=-1, keepdims=True)
    exp_scores = jnp.exp(scores - row_max)
    row_total = jnp.sum(exp_scores, axis=-1, keepdims=True)
    probs = exp_scores / row_total
    log_total = row_max + jnp.log(row_total)
    attended = (
        jnp.einsum(
            "ihst,ithd->ishd",
            probs.astype(jnp.bfloat16),
            values_all.reshape(head_shape),
            preferred_element_type=jnp.float32,
        )
        .reshape(row_count, model_width)
        .astype(jnp.bfloat16)
    )
    attn_out = jnp.dot(attended, w_proj, preferred_element_type=jnp.float32)
    middle = inputs + attn_out
    second_out, normed_two, inv_two = norm_forward(middle, gain_two, shift_two)
    moe_in = second_out.astype(jnp.bfloat16)
    logits = jnp.dot(moe_in, w_router, preferred_element_type=jnp.float32)
    gate_probs = jax.nn.softmax(logits, axis=-1)
    route_rows = routes.reshape(row_count, TOP)
    slot_dest = routing(route_rows, priority.reshape(row_count), row_valid, capacity)
    token_src = slot_sources(slot_dest, row_count, capacity, TOP)
    pair_src = slot_sources(slot_dest, row_count * TOP, capacity, 1)
    padded_in = jnp.concatenate([moe_in, jnp.zeros((1, model_width), jnp.bfloat16)], axis=0)
    arrived = send_slots(padded_in[token_src])
    w_first = expert_in.reshape(local_experts, local_hidden, model_width)
    w_second = expert_out.reshape(local_experts, local_hidden, model_width)
    pre_act = jnp.einsum("secd,efd->secf", arrived, w_first, preferred_element_type=jnp.float32)
    hidden = jax.nn.gelu(pre_act, approximate=False).astype(jnp.bfloat16)
    partial_out = jnp.einsum(
        "secf,efd->secd", hidden, w_second, preferred_element_type=jnp.float32
    ).astype(jnp.bfloat16)
    value_table = return_slots(partial_out)
    padded_values = jnp.concatenate([value_table, jnp.zeros((1, model_width), jnp.float32)], axis=0)
    pair_values = padded_values[slot_dest.reshape(-1)].reshape(row_count, TOP, model_width)
    chosen = jnp.take_along_axis(gate_probs, route_rows, axis=1)
    moe_out = jnp.sum(chosen[:, :, None] * pair_values, axis=1)
    total = middle + moe_out
    output = (total * valid_col).astype(jnp.bfloat16).reshape(image_count, patch_rows, model_width)
    stat_terms = jnp.stack(
        [
            jnp.sum(valid_col * attn_out * attn_out),
            jnp.sum(valid_col * moe_out * moe_out),
            jnp.sum(valid_col * total * total),
            jnp.sum(row_valid.astype(jnp.float32)) * model_width,
        ]
    )
    grad_total = cotangent.reshape(row_count, model_width).astype(jnp.float32) * valid_col
    grad_gate = jnp.sum(grad_total[:, None, :] * pair_values, axis=2)
    grad_value = (
        (grad_total[:, None, :] * chosen[:, :, None])
        .astype(jnp.bfloat16)
        .reshape(row_count * TOP, model_width)
    )
    padded_grad = jnp.concatenate([grad_value, jnp.zeros((1, model_width), jnp.bfloat16)], axis=0)
    grad_sent = send_slots(padded_grad[pair_src])
    grad_hidden = jnp.einsum(
        "secd,efd->secf", grad_sent, w_second, preferred_element_type=jnp.float32
    )
    grad_pre = (grad_hidden * gelu_slope(pre_act)).astype(jnp.bfloat16)
    grad_second = jnp.einsum(
        "secf,secd->efd", hidden, grad_sent, preferred_element_type=jnp.float32
    ).reshape(-1, model_width)
    grad_first = jnp.einsum(
        "secf,secd->efd", grad_pre, arrived, preferred_element_type=jnp.float32
    ).reshape(-1, model_width)
    grad_part_in = jnp.einsum(
        "secf,efd->secd", grad_pre, w_first, preferred_element_type=jnp.float32
    ).astype(jnp.bfloat16)
    grad_in_table = return_slots(grad_part_in)
    padded_back = jnp.concatenate([grad_in_table, jnp.zeros((1, model_width), jnp.float32)], axis=0)
    grad_dispatch = jnp.sum(
        padded_back[slot_dest.reshape(-1)].reshape(row_count, TOP, model_width), axis=1
    )
    expert_ids = jnp.arange(EXPERTS, dtype=jnp.int32)
    grad_probs = jnp.sum(
        jnp.where(route_rows[:, :, None] == expert_ids[None, None, :], grad_gate[:, :, None], 0.0),
        axis=1,
    )
    grad_logits = (
        gate_probs * (grad_probs - jnp.sum(grad_probs * gate_probs, axis=-1, keepdims=True))
    ).astype(jnp.bfloat16)
    grad_router = jnp.einsum("rd,re->de", moe_in, grad_logits, preferred_element_type=jnp.float32)
    grad_moe_in = grad_dispatch + jnp.einsum(
        "re,de->rd", grad_logits, w_router, preferred_element_type=jnp.float32
    )
    grad_mid_norm, grad_gain_two, grad_shift_two = norm_backward(
        grad_moe_in, normed_two, inv_two, gain_two
    )
    grad_middle = grad_total + grad_mid_norm
    grad_attn = grad_middle.astype(jnp.bfloat16)
    grad_proj = jnp.einsum("rd,re->de", attended, grad_attn, preferred_element_type=jnp.float32)
    grad_attended = jnp.einsum(
        "re,de->rd", grad_attn, w_proj, preferred_element_type=jnp.float32
    ).astype(jnp.bfloat16)
    grad_heads = grad_attended.reshape(head_shape)
    keys_again, values_again = (
        lax.all_gather(key_rows, "seq", axis=1, tiled=True),
        lax.all_gather(value_rows, "seq", axis=1, tiled=True),
    )
    key_heads = keys_again.reshape(head_shape)
    value_heads = values_again.reshape(head_shape)
    probs_again = jnp.exp(score_block(query_heads, key_heads, key_mask, score_scale) - log_total)
    grad_probs_att = jnp.einsum(
        "ishd,ithd->ihst", grad_heads, value_heads, preferred_element_type=jnp.float32
    )
    delta = jnp.sum(grad_probs_att * probs_again, axis=-1, keepdims=True)
    grad_scores = (probs_again * (grad_probs_att - delta)).astype(jnp.bfloat16)
    grad_queries = (
        jnp.einsum("ihst,ithd->ishd", grad_scores, key_heads, preferred_element_type=jnp.float32)
        * score_scale
    )
    grad_keys_full = (
        jnp.einsum("ihst,ishd->ithd", grad_scores, query_heads, preferred_element_type=jnp.float32)
        * score_scale
    )
    grad_values_full = jnp.einsum(
        "ihst,ishd->ithd",
        probs_again.astype(jnp.bfloat16),
        grad_heads,
        preferred_element_type=jnp.float32,
    )
    grad_keys, grad_values = (
        lax.psum_scatter(
            grad_keys_full.reshape(image_count, full_patches, model_width),
            "seq",
            scatter_dimension=1,
            tiled=True,
        ),
        lax.psum_scatter(
            grad_values_full.reshape(image_count, full_patches, model_width),
            "seq",
            scatter_dimension=1,
            tiled=True,
        ),
    )
    grad_packed = jnp.concatenate(
        [
            grad_queries.reshape(row_count, model_width),
            grad_keys.reshape(row_count, model_width),
            grad_values.reshape(row_count, model_width),
        ],
        axis=1,
    ).astype(jnp.bfloat16)
    grad_qkv = jnp.einsum("rd,re->de", attn_in, grad_packed, preferred_element_type=jnp.float32)
    grad_attn_in = jnp.einsum("re,de->rd", grad_packed, w_qkv, preferred_element_type=jnp.float32)
    grad_in_norm, grad_gain_one, grad_shift_one = norm_backward(
        grad_attn_in, normed_one, inv_one, gain_one
    )
    input_grad = (
        (grad_middle + grad_in_norm)
        .astype(jnp.bfloat16)
        .reshape(image_count, patch_rows, model_width)
    )
    summed = lax.psum(
        (
            grad_qkv,
            grad_proj,
            grad_router,
            grad_gain_one,
            grad_shift_one,
            grad_gain_two,
            grad_shift_two,
            stat_terms,
        ),
        ("seq", "ep"),
    )
    expert_grads = (
        lax.psum(grad_first.astype(jnp.bfloat16), "seq").astype(jnp.float32),
        lax.psum(grad_second.astype(jnp.bfloat16), "seq").astype(jnp.float32),
    )
    rms_stats = jnp.sqrt(summed[7][:3] / summed[7][3])
    return (
        output,
        input_grad,
        summed[3],
        summed[4],
        summed[0],
        summed[1],
        summed[5],
        summed[6],
        summed[2],
        expert_grads[0],
        expert_grads[1],
        rms_stats,
    )


def solution(mesh):
    in_specs = (
        P("ep", "seq", None),
        P("ep", "seq", None),
        P("ep", "seq"),
        P("ep"),
        P(),
        P(),
        P(),
        P(),
        P(),
        P(),
        P(),
        P("ep", None),
        P("ep", None),
        P("ep", "seq", None),
    )
    out_specs = (
        P("ep", "seq", None),
        P("ep", "seq", None),
        P(),
        P(),
        P(),
        P(),
        P(),
        P(),
        P(),
        P("ep", None),
        P("ep", None),
        P(),
    )
    return jax.shard_map(
        per_device, mesh=mesh, in_specs=in_specs, out_specs=out_specs, check_vma=False
    )
```

profile of v0, /device:TPU:0, one launch (start us, length us, event | category | flops | bytes accessed | tf_op | source)
XLA Modules:
  0.0 1413.0 jit_solution(5902060563627623308)
XLA Ops:
  15.6 3.3 reshape_reshape.9
  18.9 3.8 copy.111
  28.5 6.5 gather_fusion
  35.0 7.7 gather_fusion.1
  44.1 4.0 gather_fusion.2
  50.4 4.8 reduce-window.6
  65.3 5.5 scatter_custom_fusion.1
  71.5 5.4 copy.110
  76.9 5.0 fusion.69
  81.9 5.0 copy-done.1
  86.9 3.8 fusion.23
  90.7 9.3 all-gather.3.cloned.1.call-done
  100.0 5.3 copy.109
  105.3 8.2 fusion.37
  113.5 4.0 copy.112
  117.5 3.5 convert_element_type.128
  121.0 3.5 fusion.67
  127.9 6.7 gather_fusion.4
  137.0 3.6 copy.119
  140.7 5.1 all-to-all-start
  156.2 4.6 mul.269
  160.8 5.4 scatter_custom_fusion.2
  169.5 12.0 gather_fusion.8
  184.7 7.0 gather_fusion.6
  194.2 3.7 copy.124
  197.8 5.3 all-to-all-start.2
  203.2 35.2 %fusion.2 = (bf16[8,4,29,3072]{3,2,0,1:T(8,128)(2,1)S(1)}, f32[4,8,29,3072]{3,2,1,0:T(8,128)}) fusion(bf16[4,3072,768,1]{2,1,3,0:T(8,128)(2,1)} %bitcast.184, bf16[8,4,29,768]{3,1,2,0:T(4,128)(2,1)} %all-to-all-done), kind=kOutput, calls=%fused_computation.24 | convolution fusion | flops 4564156416 | bytes 37404672 | tf_op jit(solution)/shard_map/secd,efd->secf/dot_general | solution.py:184
  238.3 11.5 fusion.30
  252.0 5.6 all-to-all-start.1
  257.6 13.6 fusion.8
  271.3 11.5 fusion.31
  285.0 7.3 all-to-all-done.1
  292.3 4.3 all-to-all-start.3
  310.3 6.7 gather_fusion.5
  317.0 4.4 reshape.414
  321.4 7.5 multiply_reduce_fusion.1
  342.1 6.7 gather_fusion.7
  348.8 4.6 reshape.418
  353.4 6.0 reduce_sum.241
  359.5 5.4 fusion.41
  368.1 3.3 reshape.419
  371.4 3.8 copy.130
  375.2 14.9 %multiply_reduce_fusion = (f32[3,12,144]{2,1,0:T(8,128)S(1)}, f32[3,12,144,576]{3,2,1,0:T(8,128)}) fusion(f32[3,12,144,576]{3,2,1,0:T(8,128)} %copy-done.1, f32[3,12,144]{2,1,0:T(8,128)} %log_add_fusion, bf16[3,144,12,64]{1,3,2,0:T(8,128)(2,1)} %copy.130, bf16[3,576,12,64]{1,3,2,0:T(8,128)(2,1)} %bitcast.170), kind=kOutput, calls=%fused_computation.17 | convolution fusion | flops 391158720 | bytes 27247104 | tf_op jit(solution)/shard_map/ishd,ithd->ihst/dot_general | solution.py:260
  390.1 9.9 multiply_convert_fusion
  400.1 4.2 broadcast_multiply_fusion
  404.7 7.5 copy.133
  412.2 9.9 fusion.25
  422.1 7.5 copy.135
  429.7 12.3 bitcast_convert_fusion
  442.0 12.1 bitcast_convert_fusion.1
  454.2 8.4 fusion.38
  462.6 4.2 copy.131
  466.9 3.5 reshape.420
  472.4 3.7 fusion.44
  478.4 61.2 %reduce-scatter.5.cloned.1.call-done = f32[3,144,768]{2,1,0:T(8,128)} async-done(((f32[3,576,768]{2,1,0:T(8,128)}), f32[3,144,768]{2,1,0:T(8,128)}) %reduce-scatter.5.cloned.1.call-update) | async-done | bytes 1327120 | tf_op jit(solution)/shard_map/reduce_scatter | solution.py:286
  541.8 6.5 fusion.42
  551.5 5.5 multiply_reduce_fusion.4
  557.0 40.4 %all-reduce.7 = (f32[768]{0:T(1024)}, f32[768]{0:T(1024)}, f32[768]{0:T(1024)}, f32[768]{0:T(1024)}, f32[4]{0:T(128)}) all-reduce(f32[768]{0:T(1024)} %get-tuple-element.17, f32[768]{0:T(1024)} %get-tuple-element.26, f32[768]{0:T(1024)S(1)} %copy-done.36, f32[768]{0:T(1024)S(1)} %copy-done.37, ...), channel_id=1, replica_groups=mesh['seq'=4,'ep'=8] {'seq','ep'}, use_global_device_ids=true, to_apply=%region_27.28 | all-reduce | flops 3076 | bytes 24608 | tf_op jit(solution)/shard_map/psum | solution.py:311
  605.1 588.1 %all-reduce.15.cloned.1.call-done = (bf16[12288,768]{1,0:T(8,128)(2,1)}, bf16[12288,768]{1,0:T(8,128)(2,1)}) async-done(((bf16[12288,768]{1,0:T(8,128)(2,1)}, bf16[12288,768]{1,0:T(8,128)(2,1)}), (bf16[12288,768]{1,0:T(8,128)(2,1)}, bf16[12288,768]{1,0:T(8,128)(2,1)})) %all-reduce.15.cloned.1.call-update) | async-done | bytes 37748752 | tf_op jit(solution)/shard_map/psum | solution.py:325
  1193.2 21.1 %convert_element_type.149 = f32[12288,768]{1,0:T(8,128)} convert(bf16[12288,768]{1,0:T(8,128)(2,1)} %get-tuple-element.36) | non-fusion elementwise | flops 9437184 | bytes 56623104 | tf_op jit(solution)/shard_map/convert_element_type | solution.py:325
  1214.2 4.6 copy-done.6
  1218.9 12.9 convert_element_type.152
  1231.8 165.5 %all-reduce.13.cloned.1.call-done = (f32[768,2304]{1,0:T(8,128)}, f32[768,768]{1,0:T(8,128)}, f32[768,32]{0,1:T(8,128)}) async-done(((f32[768,2304]{1,0:T(8,128)}, f32[768,768]{1,0:T(8,128)}, f32[768,32]{0,1:T(8,128)}), (f32[768,2304]{1,0:T(8,128)}, f32[768,768]{1,0:T(8,128)}, f32[768,32]{0,1:T(8,128)})) %all-reduce.13.cloned.1.call-update) | async-done | bytes 9535504 | tf_op jit(solution)/shard_map/psum | solution.py:311
  1397.3 6.6 copy.162
  (205 shorter events, 106.9 us)
Async XLA Ops:
  7.2 4.6 copy-start
  7.2 64.3 %all-gather.5.cloned.1.call-start = ((), (), s32[]{:S(2)}) async-start(), calls=%async_computation.7 | async-start | bytes 3317760 | tf_op jit(solution)/shard_map/all_gather | solution.py:151
  10.2 3.3 copy-start.32
  10.3 3.2 copy-start.34
  11.8 1.8 copy-start.12
  14.9 85.1 %all-gather.3.cloned.1.call-start = ((), (), s32[]{:S(2)}) async-start(), calls=%async_computation.6 | async-start | bytes 3317760 | tf_op jit(solution)/shard_map/all_gather | solution.py:152
  14.9 8.9 copy-start.31
  15.6 9.1 copy-start.44
  24.8 0.6 copy-start.41
  49.0 6.3 copy-start.43
  65.3 5.5 copy-start.39
  81.9 5.0 copy-start.1
  81.9 5.0 copy-start.17
  121.0 4.5 copy-start.23
  121.0 4.5 copy-start.42
  124.5 1.1 copy-start.3
  124.5 1.3 copy-start.19
  125.6 0.6 copy-start.27
  126.1 0.9 copy-start.8
  140.7 57.1 %all-to-all-start = ((bf16[8,4,29,768]{3,1,2,0:T(4,128)(2,1)}), bf16[8,4,29,768]{3,1,2,0:T(4,128)(2,1)}, u32[]{:S(2)}, u32[]{:S(2)}) async-start(bf16[8,4,29,768]{3,1,2,0:T(4,128)(2,1)} %copy.119), calls=%async_computation | async-start | bytes 2850816 | tf_op jit(solution)/shard_map/all_to_all | solution.py:126
  146.5 9.8 copy-start.25
  152.7 1.1 copy-start.7
  167.7 0.6 copy-start.15
  167.7 0.6 copy-start.21
  168.3 0.6 copy-start.29
  169.5 12.0 copy-start.38
  197.8 54.2 %all-to-all-start.2 = ((bf16[8,4,29,768]{3,1,2,0:T(4,128)(2,1)}), bf16[8,4,29,768]{3,1,2,0:T(4,128)(2,1)}, u32[]{:S(2)}, u32[]{:S(2)}) async-start(bf16[8,4,29,768]{3,1,2,0:T(4,128)(2,1)} %copy.124), calls=%async_computation.2 | async-start | bytes 2850816 | tf_op jit(solution)/shard_map/all_to_all | solution.py:126
  238.3 11.5 copy-start.46
  252.0 40.3 %all-to-all-start.1 = ((bf16[8,4,29,768]{3,1,2,0:T(4,128)(2,1)}), bf16[8,4,29,768]{3,1,2,0:T(4,128)(2,1)}, u32[]{:S(2)}, u32[]{:S(2)}) async-start(bf16[8,4,29,768]{3,1,2,0:T(4,128)(2,1)} %copy.121), calls=%async_computation.1 | async-start | bytes 2850816 | tf_op jit(solution)/shard_map/all_to_all | solution.py:129
  271.3 11.5 copy-start.45
  282.8 15.0 %copy-start.40 = (s32[864]{0:T(1024)S(1)}, s32[864]{0:T(1024)}, u32[]{:S(2)}) copy-start(s32[864]{0:T(1024)} %copy-done.39) | copy-start | bytes 10372
  292.3 41.4 %all-to-all-start.3 = ((bf16[8,4,29,768]{3,1,2,0:T(4,128)(2,1)}), bf16[8,4,29,768]{3,1,2,0:T(4,128)(2,1)}, u32[]{:S(2)}, u32[]{:S(2)}) async-start(bf16[8,4,29,768]{3,1,2,0:T(4,128)(2,1)} %copy.126), calls=%async_computation.3 | async-start | bytes 2850816 | tf_op jit(solution)/shard_map/all_to_all | solution.py:129
  296.6 179.5 %reduce-scatter.3.cloned.1.call-start = ((), (), s32[]{:S(2)}) async-start(), calls=%async_computation.8 | async-start | bytes 6635520 | tf_op jit(solution)/shard_map/reduce_scatter | solution.py:280
  321.4 9.9 copy-start.22
  321.4 9.9 copy-start.30
  353.4 6.0 copy-start.20
  353.4 6.0 copy-start.24
  353.4 6.0 copy-start.26
  353.4 6.0 copy-start.28
  359.4 5.5 copy-start.4
  359.4 5.4 copy-start.11
  364.9 1.7 copy-start.10
  365.4 1.1 copy-start.5
  375.2 14.9 %copy-start.16 = (f32[3,12,144]{2,1,0:T(8,128)S(1)}, f32[3,12,144]{2,1,0:T(8,128)}, u32[]{:S(2)}) copy-start(f32[3,12,144]{2,1,0:T(8,128)} %log_add_fusion) | copy-start | bytes 62212
  390.1 9.9 copy-start.9
  400.1 4.6 copy-start.2
  412.1 127.4 %reduce-scatter.5.cloned.1.call-start = ((), (), s32[]{:S(2)}) async-start(), calls=%async_computation.9 | async-start | bytes 6635520 | tf_op jit(solution)/shard_map/reduce_scatter | solution.py:286
  429.7 763.5 %all-reduce.15.cloned.1.call-start = ((), (), s32[]{:S(2)}) async-start(), calls=%async_computation.11 | async-start | bytes 75497472 | tf_op jit(solution)/shard_map/psum | solution.py:325
  454.2 943.1 %all-reduce.13.cloned.1.call-start = ((), (), s32[]{:S(2)}) async-start(), calls=%async_computation.10 | async-start | bytes 19070976 | tf_op jit(solution)/shard_map/psum | solution.py:311
  540.9 0.8 copy-start.13
  548.3 3.2 copy-start.33
  548.3 3.2 copy-start.35
  551.5 5.5 copy-start.36
  551.5 5.5 copy-start.37
  1193.2 25.7 %copy-start.6 = (bf16[12288,768]{1,0:T(8,128)(2,1)S(1)}, bf16[12288,768]{1,0:T(8,128)(2,1)}, u32[]{:S(2)}) copy-start(bf16[12288,768]{1,0:T(8,128)(2,1)} %get-tuple-element.37) | copy-start | bytes 56623108
  1397.3 6.6 copy-start.14
  1403.9 1.4 copy-start.18
Sparse Core Ops, SparseCore 0:
  15.0 42.6 all-gather.4
  60.1 39.9 all-gather.2
  412.3 62.3 reduce-scatter.2
  477.5 61.9 reduce-scatter.4
  543.7 649.4 all-reduce.14
  1201.5 195.7 all-reduce.12
where the time goes:
time: 1420 us; the launch traced here: 1410 us
  waiting for transfers between devices  832 us (59%)
  local copies, waits for them, and re-layouts  215 us (15%)
  matrix products  178 us (13%)
  other arithmetic  110 us (8%)
  blocking collectives  40.4 us (3%)
  starting transfers between devices  20.5 us (1%)
  between operations  16.3 us (1%)
    psum x1, waiting for transfers between devices, per_device(): lax.psum(grad_first.astype(jnp.bfloat16), 'seq').astype(jnp.float32)  588 us
    psum x1, waiting for transfers between devices, per_device(): lax.psum((grad_qkv, grad_proj, grad_router, grad_gain_one, grad_shift_one...  165 us
    reduce_scatter x1, waiting for transfers between devices, per_device(): lax.psum_scatter(grad_values_full.reshape(image_count, full_patches, mode...  61.2 us
    psum x1, blocking collectives, per_device(): lax.psum((grad_qkv, grad_proj, grad_router, grad_gain_one, grad_shift_one...  40.4 us
    dot_general x1, matrix products, per_device(): jnp.einsum('secd,efd->secf', arrived, w_first, preferred_element_type=jnp...  35.2 us
  transfers between devices with their start and end apart: 10, of which 5 were waited for; matrix products, arithmetic and copies ran while one was open for 25% of the time, Pallas kernels for 0%

commit v1 on v0

--- a/solution.py
+++ b/solution.py
@@ -309,17 +309,20 @@
         .reshape(image_count, patch_rows, model_width)
     )
     summed = lax.psum(
-        (
-            grad_qkv,
-            grad_proj,
-            grad_router,
-            grad_gain_one,
-            grad_shift_one,
-            grad_gain_two,
-            grad_shift_two,
-            stat_terms,
+        lax.psum(
+            (
+                grad_qkv,
+                grad_proj,
+                grad_router,
+                grad_gain_one,
+                grad_shift_one,
+                grad_gain_two,
+                grad_shift_two,
+                stat_terms,
+            ),
+            "ep",
         ),
-        ("seq", "ep"),
+        "seq",
     )
     expert_grads = (
         lax.psum(grad_first.astype(jnp.bfloat16), "seq").astype(jnp.float32),

time: 1420 us -> 1620 us (1.14)
  waiting for transfers between devices: 832 us -> 1030 us
    psum x0 -> x1, waiting for transfers between devices: none -> 159 us  [per_device(): lax.psum(lax.psum((grad_qkv, grad_proj, grad_router, grad_gain_one, grad_...]
    reduce_scatter x1, waiting for transfers between devices: 0.01 us -> 23.9 us  [per_device(): lax.psum_scatter(grad_keys_full.reshape(image_count, full_patches, model_...]
    psum x0 -> x1, blocking collectives: none -> 18.3 us  [per_device(): lax.psum(lax.psum((grad_qkv, grad_proj, grad_router, grad_gain_one, grad_...]
  transfers between devices with their start and end apart: 10 -> 11, of which waited for: 5 -> 7; matrix products, arithmetic and copies ran while one was open for 25% -> 21% of each run, Pallas kernels for 0% -> 0%
where the time goes in v1:
time: 1620 us; the launch traced here: 1610 us
  waiting for transfers between devices  1030 us (64%)
  local copies, waits for them, and re-layouts  215 us (13%)
  matrix products  178 us (11%)
  other arithmetic  110 us (7%)
  blocking collectives  47.2 us (3%)
  starting transfers between devices  20.5 us (1%)
  between operations  16.3 us (1%)
    psum x1, waiting for transfers between devices, per_device(): lax.psum(grad_first.astype(jnp.bfloat16), 'seq').astype(jnp.float32)  591 us
    psum x1, waiting for transfers between devices, per_device(): lax.psum((grad_qkv, grad_proj, grad_router, grad_gain_one, grad_shift_one...  174 us
    psum x1, waiting for transfers between devices, per_device(): lax.psum(lax.psum((grad_qkv, grad_proj, grad_router, grad_gain_one, grad_...  159 us
    reduce_scatter x1, waiting for transfers between devices, per_device(): lax.psum_scatter(grad_values_full.reshape(image_count, full_patches, mode...  63.2 us
    dot_general x1, matrix products, per_device(): jnp.einsum('secd,efd->secf', arrived, w_first, preferred_element_type=jnp...  35.2 us
  transfers between devices with their start and end apart: 11, of which 7 were waited for; matrix products, arithmetic and copies ran while one was open for 21% of the time, Pallas kernels for 0%

profile of v1, /device:TPU:0, one launch (start us, length us, event | category | flops | bytes accessed | tf_op | source)
XLA Modules:
  0.0 1614.5 jit_solution(942727287853634670)
XLA Ops:
  18.9 3.8 copy.111
  28.5 6.5 gather_fusion
  35.0 7.7 gather_fusion.1
  44.1 4.0 gather_fusion.2
  50.4 4.8 reduce-window.6
  65.3 5.5 scatter_custom_fusion.1
  71.5 5.4 copy.110
  76.9 5.0 fusion.69
  81.9 5.0 copy-done.1
  86.9 3.8 fusion.23
  90.7 9.3 all-gather.3.cloned.1.call-done
  100.0 5.3 copy.109
  105.3 8.2 fusion.37
  113.5 4.0 copy.112
  117.5 3.5 convert_element_type.128
  127.9 6.7 gather_fusion.4
  137.1 3.6 copy.119
  140.7 5.1 all-to-all-start
  156.3 4.6 mul.269
  160.9 5.4 scatter_custom_fusion.2
  169.6 12.0 gather_fusion.8
  184.8 7.0 gather_fusion.6
  194.3 3.7 copy.124
  197.9 5.3 all-to-all-start.2
  203.3 35.2 %fusion.2 = (bf16[8,4,29,3072]{3,2,0,1:T(8,128)(2,1)S(1)}, f32[4,8,29,3072]{3,2,1,0:T(8,128)}) fusion(bf16[4,3072,768,1]{2,1,3,0:T(8,128)(2,1)} %bitcast.184, bf16[8,4,29,768]{3,1,2,0:T(4,128)(2,1)} %all-to-all-done), kind=kOutput, calls=%fused_computation.24 | convolution fusion | flops 4564156416 | bytes 37404672 | tf_op jit(solution)/shard_map/secd,efd->secf/dot_general | solution.py:184
  238.4 11.5 fusion.30
  252.1 5.6 all-to-all-start.1
  257.7 13.6 fusion.8
  271.3 11.5 fusion.31
  285.1 7.3 all-to-all-done.1
  292.4 4.3 all-to-all-start.3
  310.4 6.7 gather_fusion.5
  317.1 4.4 reshape.414
  321.5 7.5 multiply_reduce_fusion.1
  342.2 6.7 gather_fusion.7
  348.9 4.6 reshape.418
  353.5 6.0 reduce_sum.241
  359.5 5.4 fusion.41
  371.4 3.8 copy.130
  375.2 14.9 multiply_reduce_fusion
  390.2 9.9 multiply_convert_fusion
  400.1 4.2 broadcast_multiply_fusion
  404.7 7.5 copy.133
  412.3 9.9 fusion.25
  422.2 7.5 copy.135
  429.8 7.7 fusion.38
  437.5 4.0 copy.131
  441.5 3.5 reshape.420
  446.9 3.8 fusion.44
  450.8 23.9 %reduce-scatter.3.cloned.1.call-done = f32[3,144,768]{2,1,0:T(8,128)} async-done(((f32[3,576,768]{2,1,0:T(8,128)}), f32[3,144,768]{2,1,0:T(8,128)}) %reduce-scatter.3.cloned.1.call-update) | async-done | bytes 1327120 | tf_op jit(solution)/shard_map/reduce_scatter | solution.py:280
  477.0 63.2 %reduce-scatter.5.cloned.1.call-done = f32[3,144,768]{2,1,0:T(8,128)} async-done(((f32[3,576,768]{2,1,0:T(8,128)}), f32[3,144,768]{2,1,0:T(8,128)}) %reduce-scatter.5.cloned.1.call-update) | async-done | bytes 1327120 | tf_op jit(solution)/shard_map/reduce_scatter | solution.py:286
  542.4 6.5 fusion.42
  549.0 12.4 bitcast_convert_fusion
  561.3 12.1 bitcast_convert_fusion.1
  573.5 173.9 %all-reduce.16.cloned.1.call-done = (f32[768,2304]{1,0:T(8,128)}, f32[768,768]{1,0:T(8,128)}, f32[768,32]{0,1:T(8,128)}) async-done(((f32[768,2304]{1,0:T(8,128)}, f32[768,768]{1,0:T(8,128)}, f32[768,32]{0,1:T(8,128)}), (f32[768,2304]{1,0:T(8,128)}, f32[768,768]{1,0:T(8,128)}, f32[768,32]{0,1:T(8,128)})) %all-reduce.16.cloned.1.call-update) | async-done | bytes 9535504 | tf_op jit(solution)/shard_map/psum | solution.py:312
  750.6 5.5 multiply_reduce_fusion.4
  756.1 28.9 %all-reduce.7 = (f32[768]{0:T(1024)}, f32[768]{0:T(1024)}, f32[768]{0:T(1024)}, f32[768]{0:T(1024)}, f32[4]{0:T(128)}) all-reduce(f32[768]{0:T(1024)} %get-tuple-element.17, f32[768]{0:T(1024)} %get-tuple-element.26, f32[768]{0:T(1024)S(1)} %copy-done.36, f32[768]{0:T(1024)S(1)} %copy-done.37, ...), channel_id=1, replica_groups=mesh['seq'=4,'ep'=8] {'ep'}, use_global_device_ids=true, to_apply=%region_27.28 | all-reduce | flops 3076 | bytes 24608 | tf_op jit(solution)/shard_map/psum | solution.py:312
  785.0 18.3 %all-reduce.9 = (f32[768]{0:T(1024)}, f32[768]{0:T(1024)}, f32[768]{0:T(1024)}, f32[768]{0:T(1024)}, f32[4]{0:T(128)S(1)}) all-reduce(f32[768]{0:T(1024)} %get-tuple-element.28, f32[768]{0:T(1024)} %get-tuple-element.29, f32[768]{0:T(1024)} %get-tuple-element.30, ...), channel_id=1, replica_groups=mesh['seq'=4,'ep'=8] {'seq'}, use_global_device_ids=true, to_apply=%region_28.29 | all-reduce | flops 3076 | bytes 24608 | tf_op jit(solution)/shard_map/psum | solution.py:311
  809.7 591.4 %all-reduce.20.cloned.1.call-done = (bf16[12288,768]{1,0:T(8,128)(2,1)}, bf16[12288,768]{1,0:T(8,128)(2,1)}) async-done(((bf16[12288,768]{1,0:T(8,128)(2,1)}, bf16[12288,768]{1,0:T(8,128)(2,1)}), (bf16[12288,768]{1,0:T(8,128)(2,1)}, bf16[12288,768]{1,0:T(8,128)(2,1)})) %all-reduce.20.cloned.1.call-update) | async-done | bytes 37748752 | tf_op jit(solution)/shard_map/psum | solution.py:328
  1401.1 21.0 %convert_element_type.149 = f32[12288,768]{1,0:T(8,128)} convert(bf16[12288,768]{1,0:T(8,128)(2,1)} %get-tuple-element.44) | non-fusion elementwise | flops 9437184 | bytes 56623104 | tf_op jit(solution)/shard_map/convert_element_type | solution.py:328
  1422.1 4.8 copy-done.6
  1427.0 13.0 convert_element_type.152
  1440.0 158.8 %all-reduce.18.cloned.1.call-done = (f32[768,2304]{1,0:T(8,128)}, f32[768,768]{1,0:T(8,128)}, f32[768,32]{0,1:T(8,128)}) async-done(((f32[768,2304]{1,0:T(8,128)}, f32[768,768]{1,0:T(8,128)}, f32[768,32]{0,1:T(8,128)}), (f32[768,2304]{1,0:T(8,128)}, f32[768,768]{1,0:T(8,128)}, f32[768,32]{0,1:T(8,128)})) %all-reduce.18.cloned.1.call-update) | async-done | bytes 9535504 | tf_op jit(solution)/shard_map/psum | solution.py:311
  1598.8 6.6 copy.165
  (209 shorter events, 115.7 us)
Async XLA Ops:
  7.2 4.6 copy-start
  7.2 64.3 %all-gather.5.cloned.1.call-start = ((), (), s32[]{:S(2)}) async-start(), calls=%async_computation.7 | async-start | bytes 3317760 | tf_op jit(solution)/shard_map/all_gather | solution.py:151
  10.2 3.3 copy-start.32
  10.3 3.2 copy-start.34
  11.8 1.8 copy-start.12
  14.9 85.1 %all-gather.3.cloned.1.call-start = ((), (), s32[]{:S(2)}) async-start(), calls=%async_computation.6 | async-start | bytes 3317760 | tf_op jit(solution)/shard_map/all_gather | solution.py:152
  14.9 9.0 copy-start.31
  15.6 9.1 copy-start.44
  24.8 0.6 copy-start.41
  49.0 6.3 copy-start.43
  65.3 5.5 copy-start.39
  81.9 5.0 copy-start.1
  81.9 5.0 copy-start.17
  121.0 4.6 copy-start.23
  121.0 4.6 copy-start.42
  124.5 1.1 copy-start.3
  124.5 1.4 copy-start.19
  125.6 0.6 copy-start.27
  126.2 0.9 copy-start.8
  140.7 57.2 %all-to-all-start = ((bf16[8,4,29,768]{3,1,2,0:T(4,128)(2,1)}), bf16[8,4,29,768]{3,1,2,0:T(4,128)(2,1)}, u32[]{:S(2)}, u32[]{:S(2)}) async-start(bf16[8,4,29,768]{3,1,2,0:T(4,128)(2,1)} %copy.119), calls=%async_computation | async-start | bytes 2850816 | tf_op jit(solution)/shard_map/all_to_all | solution.py:126
  146.5 9.8 copy-start.25
  152.8 1.1 copy-start.7
  167.8 0.6 copy-start.15
  167.8 0.6 copy-start.21
  168.4 0.6 copy-start.29
  169.6 12.0 copy-start.38
  197.9 54.2 %all-to-all-start.2 = ((bf16[8,4,29,768]{3,1,2,0:T(4,128)(2,1)}), bf16[8,4,29,768]{3,1,2,0:T(4,128)(2,1)}, u32[]{:S(2)}, u32[]{:S(2)}) async-start(bf16[8,4,29,768]{3,1,2,0:T(4,128)(2,1)} %copy.124), calls=%async_computation.2 | async-start | bytes 2850816 | tf_op jit(solution)/shard_map/all_to_all | solution.py:126
  238.4 11.5 copy-start.46
  252.1 40.3 %all-to-all-start.1 = ((bf16[8,4,29,768]{3,1,2,0:T(4,128)(2,1)}), bf16[8,4,29,768]{3,1,2,0:T(4,128)(2,1)}, u32[]{:S(2)}, u32[]{:S(2)}) async-start(bf16[8,4,29,768]{3,1,2,0:T(4,128)(2,1)} %copy.121), calls=%async_computation.1 | async-start | bytes 2850816 | tf_op jit(solution)/shard_map/all_to_all | solution.py:129
  271.3 11.5 copy-start.45
  282.8 15.0 copy-start.40
  292.4 41.3 %all-to-all-start.3 = ((bf16[8,4,29,768]{3,1,2,0:T(4,128)(2,1)}), bf16[8,4,29,768]{3,1,2,0:T(4,128)(2,1)}, u32[]{:S(2)}, u32[]{:S(2)}) async-start(bf16[8,4,29,768]{3,1,2,0:T(4,128)(2,1)} %copy.126), calls=%async_computation.3 | async-start | bytes 2850816 | tf_op jit(solution)/shard_map/all_to_all | solution.py:129
  296.7 178.0 %reduce-scatter.3.cloned.1.call-start = ((), (), s32[]{:S(2)}) async-start(), calls=%async_computation.8 | async-start | bytes 6635520 | tf_op jit(solution)/shard_map/reduce_scatter | solution.py:280
  321.5 9.8 copy-start.22
  321.5 9.8 copy-start.30
  353.5 6.0 copy-start.20
  353.5 6.0 copy-start.24
  353.5 6.0 copy-start.26
  353.5 6.0 copy-start.28
  359.5 5.5 copy-start.4
  359.5 5.4 copy-start.11
  364.9 1.7 copy-start.10
  365.5 1.1 copy-start.5
  375.2 14.9 copy-start.16
  390.2 9.9 copy-start.9
  400.1 4.6 copy-start.2
  412.2 127.9 %reduce-scatter.5.cloned.1.call-start = ((), (), s32[]{:S(2)}) async-start(), calls=%async_computation.9 | async-start | bytes 6635520 | tf_op jit(solution)/shard_map/reduce_scatter | solution.py:286
  429.7 317.7 %all-reduce.16.cloned.1.call-start = ((), (), s32[]{:S(2)}) async-start(), calls=%async_computation.10 | async-start | bytes 19070976 | tf_op jit(solution)/shard_map/psum | solution.py:312
  541.5 0.8 copy-start.13
  548.9 852.2 %all-reduce.20.cloned.1.call-start = ((), (), s32[]{:S(2)}) async-start(), calls=%async_computation.12 | async-start | bytes 75497472 | tf_op jit(solution)/shard_map/psum | solution.py:328
  573.5 1025.3 %all-reduce.18.cloned.1.call-start = ((), (), s32[]{:S(2)}) async-start(), calls=%async_computation.11 | async-start | bytes 19070976 | tf_op jit(solution)/shard_map/psum | solution.py:311
  747.4 3.2 copy-start.33
  747.4 3.2 copy-start.35
  750.6 5.5 copy-start.36
  750.6 5.5 copy-start.37
  1401.1 25.9 %copy-start.6 = (bf16[12288,768]{1,0:T(8,128)(2,1)S(1)}, bf16[12288,768]{1,0:T(8,128)(2,1)}, u32[]{:S(2)}) copy-start(bf16[12288,768]{1,0:T(8,128)(2,1)} %get-tuple-element.45) | copy-start | bytes 56623108
  1598.8 6.6 copy-start.14
  1605.4 1.4 copy-start.18
Sparse Core Ops, SparseCore 0:
  15.0 42.6 all-gather.4
  60.1 39.9 all-gather.2
  412.3 62.3 reduce-scatter.2
  478.1 61.9 reduce-scatter.4
  549.0 198.3 all-reduce.15
  752.1 648.9 all-reduce.19
  1405.0 193.7 all-reduce.17
